TPU v7x, 256 devices: a whole 4x4x8 slice. The times are simulated.
256 devices in a mesh: dp: 32 (over y, x, core), filter: 8 (over z).
Axes of the slice: x: 4, y: 4, z: 8, core: 2. Of those that a mesh axis runs over, the one named last changes fastest.
Arguments:
- inputs: bfloat16 [32, 48, 24, 1024], P('dp', None, None, 'filter'), may hold values from -6 to 6
- kernel: bfloat16 [3, 3, 1024, 1024], P(None, None, 'filter'), may hold values from -0.0625 to 0.0625
- cotangent: bfloat16 [32, 48, 24, 1024], P('dp', 'filter'), may hold values from -6 to 6
Outputs:
- outputs: bfloat16 [32, 48, 24, 1024], P('dp', 'filter')
- input_grad: bfloat16 [32, 48, 24, 1024], P('dp', None, None, 'filter')
- kernel_grad: float32 [1024, 3, 3, 1024], P('dp', None, None, 'filter')
All inputs are finite; a program needn't handle non-finite values.
Results may differ from a plain program's by a relative error of at most 0.001.
Values may be sent and summed in bfloat16 or wider, within the bound.
No kernel may reach another device: no remote copies, remote signals or barrier semaphores. Data moves between devices by JAX's collectives and lax.ppermute only.
A program may use at most 128 MiB of HBM per device.

v0:
```python
import jax
import jax.numpy as jnp
from jax import lax
from jax.sharding import PartitionSpec as P


def conv_rows(xpad, weights, count, width):
    total = jnp.zeros((count, width, weights.shape[3]), jnp.float32)
    for a in range(3):
        for b in range(3):
            total = total + jnp.einsum(
                "hwi,io->hwo",
                xpad[a : a + count, b : b + width],
                weights[a, b],
                preferred_element_type=jnp.float32,
            )
    return total


def on_device(inputs, kernel, cotangent):
    sample = inputs[0]
    height = sample.shape[0]
    width = sample.shape[1]
    local_in = sample.shape[2]
    channels = kernel.shape[3]
    groups = lax.axis_size("filter")
    my_rows = height // groups
    xpad = jnp.pad(sample, ((1, 1), (1, 1), (0, 0)))
    summed = lax.psum_scatter(
        conv_rows(xpad, kernel, my_rows * lax.axis_size("filter"), width),
        "filter",
        scatter_dimension=0,
        tiled=True,
    )
    outputs = summed.astype(jnp.bfloat16)[None]
    start = jnp.int32(0)
    back_pad = jnp.zeros((height + 2, width + 2, local_in), jnp.float32)
    grad_rows = lax.all_gather(cotangent, "filter", axis=1, tiled=True)[0]
    count = grad_rows.shape[0]
    taps = []
    for a in range(3):
        for b in range(3):
            contrib = jnp.einsum(
                "hwo,io->hwi", grad_rows, kernel[a, b], preferred_element_type=jnp.float32
            )
            region = lax.dynamic_slice(back_pad, (start + a, b, 0), (count, width, local_in))
            back_pad = lax.dynamic_update_slice(back_pad, region + contrib, (start + a, b, 0))
            taps.append(
                jnp.einsum(
                    "hwi,hwo->oi",
                    xpad[a : a + count, b : b + width],
                    grad_rows,
                    preferred_element_type=jnp.float32,
                )
            )
    grads = jnp.stack(taps, 1).reshape(channels, 3, 3, local_in)
    back_pad, grads = (back_pad, grads)
    input_grad = back_pad[1:-1, 1:-1].astype(jnp.bfloat16)[None]
    samples = lax.axis_size("dp")
    scale = 1.0 / jnp.sqrt(jnp.float32(samples * height * width))
    whole = lax.psum(grads, "dp")
    share = channels // samples
    mine = lax.dynamic_slice_in_dim(whole, lax.axis_index("dp") * share, share, 0)
    return (outputs, input_grad, mine * scale)


def solution(mesh):
    return jax.shard_map(
        on_device,
        mesh=mesh,
        in_specs=(
            P("dp", None, None, "filter"),
            P(None, None, "filter", None),
            P("dp", "filter", None, None),
        ),
        out_specs=(
            P("dp", "filter", None, None),
            P("dp", None, None, "filter"),
            P("dp", None, None, "filter"),
        ),
        check_vma=False,
    )
```

profile of v0, /device:TPU:1, one launch (start us, length us, event | category | flops | bytes accessed | tf_op | source)
XLA Modules:
  0.0 268.3 jit_solution(1624768555959365311)
XLA Ops:
  8.0 4.1 %fusion.124 = f32[48,24,1024]{2,1,0:T(8,128)} fusion(bf16[3,3,128,1024]{3,2,1,0:T(8,128)(2,1)} %param.4, bf16[48,24,128]{2,1,0:T(8,128)(2,1)} %bitcast.236), kind=kOutput, calls=%fused_computation.79 | convolution fusion | flops 301989888 | bytes 5275648 | tf_op jit(solution)/shard_map/hwi,io->hwo/dot_general | solution.py:11
  12.0 3.8 %fusion.127 = f32[48,24,1024]{2,1,0:T(8,128)} fusion(bf16[3,3,128,1024]{3,2,1,0:T(8,128)(2,1)} %param.4, bf16[48,24,128]{2,1,0:T(8,128)(2,1)S(1)} %bitcast.237), kind=kOutput, calls=%fused_computation.82 | convolution fusion | flops 301989888 | bytes 5275648 | tf_op jit(solution)/shard_map/hwi,io->hwo/dot_general | solution.py:11
  15.8 3.9 %fusion.130 = f32[48,24,1024]{2,1,0:T(8,128)} fusion(bf16[3,3,128,1024]{3,2,1,0:T(8,128)(2,1)} %param.4, bf16[48,24,128]{2,1,0:T(8,128)(2,1)S(1)} %bitcast.238), kind=kOutput, calls=%fused_computation.85 | convolution fusion | flops 301989888 | bytes 5275648 | tf_op jit(solution)/shard_map/hwi,io->hwo/dot_general | solution.py:11
  19.8 3.9 %fusion.136 = f32[48,24,1024]{2,1,0:T(8,128)} fusion(bf16[3,3,128,1024]{3,2,1,0:T(8,128)(2,1)} %param.4, bf16[48,24,128]{2,1,0:T(8,128)(2,1)S(1)} %bitcast.239), kind=kOutput, calls=%fused_computation.91 | convolution fusion | flops 301989888 | bytes 5275648 | tf_op jit(solution)/shard_map/hwi,io->hwo/dot_general | solution.py:11
  23.6 3.9 %fusion.139 = f32[48,24,1024]{2,1,0:T(8,128)} fusion(bf16[3,3,128,1024]{3,2,1,0:T(8,128)(2,1)} %param.4, bf16[48,24,128]{2,1,0:T(8,128)(2,1)S(1)} %bitcast.240), kind=kOutput, calls=%fused_computation.94 | convolution fusion | flops 301989888 | bytes 5275648 | tf_op jit(solution)/shard_map/hwi,io->hwo/dot_general | solution.py:11
  27.5 24.7 %all-gather.2.cloned.1.call-done = bf16[1,48,24,1024]{3,2,0,1:T(8,128)(2,1)} async-done(((bf16[1,6,24,1024]{3,2,0,1:T(8,128)(2,1)}), bf16[1,48,24,1024]{3,2,0,1:T(8,128)(2,1)}) %all-gather.2.cloned.1.call-update) | async-done | bytes 2359312 | tf_op jit(solution)/shard_map/all_gather | solution.py:38
  52.3 3.2 %fusion.69 = f32[1024,9,128]{0,2,1:T(8,128)} fusion(bf16[1,48,24,1024]{3,2,0,1:T(8,128)(2,1)} %all-gather.2.cloned.1.call-done, bf16[48,24,128]{2,1,0:T(8,128)(2,1)S(1)} %bitcast.241), kind=kOutput, calls=%fused_computation.48 | convolution fusion | flops 301989888 | bytes 3178496 | tf_op jit(solution)/shard_map/hwi,hwo->oi/dot_general | solution.py:49
  64.9 1.4 fusion.117
  66.3 6.0 %copy.46 = f32[1024,3,3,128]{3,0,2,1:T(8,128)} copy(f32[1024,3,3,128]{0,3,2,1:T(8,128)} %bitcast.58) | data formatting | bytes 9437184 | tf_op jit(solution)/shard_map/reshape | solution.py:56
  72.4 4.2 %fusion.145 = f32[48,24,1024]{2,1,0:T(8,128)} fusion(bf16[3,3,128,1024]{3,2,1,0:T(8,128)(2,1)} %param.4, bf16[48,24,128]{2,1,0:T(8,128)(2,1)S(1)} %bitcast.249), kind=kOutput, calls=%fused_computation.100 | convolution fusion | flops 301989888 | bytes 5275648 | tf_op jit(solution)/shard_map/hwi,io->hwo/dot_general | solution.py:11
  76.6 4.0 %fusion.142 = f32[48,24,1024]{2,1,0:T(8,128)} fusion(bf16[3,3,128,1024]{3,2,1,0:T(8,128)(2,1)} %param.4, bf16[48,24,128]{2,1,0:T(8,128)(2,1)S(1)} %bitcast.250), kind=kOutput, calls=%fused_computation.97 | convolution fusion | flops 301989888 | bytes 5275648 | tf_op jit(solution)/shard_map/hwi,io->hwo/dot_general | solution.py:11
  80.6 3.9 %fusion.133 = f32[48,24,1024]{2,1,0:T(8,128)} fusion(bf16[3,3,128,1024]{3,2,1,0:T(8,128)(2,1)} %param.4, bf16[1,48,24,128]{3,2,1,0:T(8,128)(2,1)S(1)} %copy-done.1), kind=kOutput, calls=%fused_computation.88 | convolution fusion | flops 301989888 | bytes 5275648 | tf_op jit(solution)/shard_map/hwi,io->hwo/dot_general | solution.py:11
  84.6 13.1 %add_add_fusion = f32[48,24,1024]{2,1,0:T(8,128)} fusion(f32[48,24,1024]{2,1,0:T(8,128)S(1)} %bitcast.253, f32[48,24,1024]{2,1,0:T(8,128)S(1)} %bitcast.255, f32[48,24,1024]{2,1,0:T(8,128)} %fusion.130, f32[48,24,1024]{2,1,0:T(8,128)} %fusion.133, f32[48,24,1024]{2,1,0:T(8,128)} %fusion.136, f32[48,24,1024]{2,1,0:T(8,128)} %fusion.139, ...), kind=kOutput, calls=%fused_computation | convolution fusion | flops 311427072 | bytes 43024384 | tf_op jit(solution)/shard_map/hwi,io->hwo/dot_general | solution.py:11
  97.7 1.7 fusion.34
  99.6 2.6 fusion.36
  102.1 6.3 %dynamic_update_slice.28 = f32[50,26,128]{2,1,0:T(8,128)S(1)} dynamic-update-slice(f32[50,26,128]{2,1,0:T(8,128)S(1)} %dynamic_update_slice.27, f32[48,24,128]{2,1,0:T(8,128)} %fusion.36, s32[]{:T(128)} %constant.5.clone.1, s32[]{:T(128)} %constant.6.clone.1, s32[]{:T(128)} %constant.5.clone.1) | dynamic-update-slice | bytes 1179652 | tf_op jit(solution)/shard_map/dynamic_update_slice | solution.py:47
  108.5 2.6 fusion.39
  111.0 6.3 %dynamic_update_slice.29 = f32[50,26,128]{2,1,0:T(8,128)S(1)} dynamic-update-slice(f32[50,26,128]{2,1,0:T(8,128)S(1)} %dynamic_update_slice.28, f32[48,24,128]{2,1,0:T(8,128)} %fusion.39, s32[]{:T(128)} %constant.5.clone.1, s32[]{:T(128)} %constant.7.clone.1, s32[]{:T(128)} %constant.5.clone.1) | dynamic-update-slice | bytes 1179652 | tf_op jit(solution)/shard_map/dynamic_update_slice | solution.py:47
  117.3 1.9 fusion.45
  119.2 2.6 fusion.48
  121.8 6.3 %dynamic_update_slice.31 = f32[50,26,128]{2,1,0:T(8,128)S(1)} dynamic-update-slice(f32[50,26,128]{2,1,0:T(8,128)S(1)} %fusion.45, f32[48,24,128]{2,1,0:T(8,128)} %fusion.48, s32[]{:T(128)} %constant.6.clone.1, s32[]{:T(128)} %constant.6.clone.1, s32[]{:T(128)} %constant.5.clone.1) | dynamic-update-slice | bytes 1179652 | tf_op jit(solution)/shard_map/dynamic_update_slice | solution.py:47
  128.1 2.6 fusion.51
  130.6 6.3 %dynamic_update_slice.32 = f32[50,26,128]{2,1,0:T(8,128)S(1)} dynamic-update-slice(f32[50,26,128]{2,1,0:T(8,128)S(1)} %dynamic_update_slice.31, f32[48,24,128]{2,1,0:T(8,128)} %fusion.51, s32[]{:T(128)} %constant.6.clone.1, s32[]{:T(128)} %constant.7.clone.1, s32[]{:T(128)} %constant.5.clone.1) | dynamic-update-slice | bytes 1179652 | tf_op jit(solution)/shard_map/dynamic_update_slice | solution.py:47
  136.9 1.8 fusion.57
  138.8 2.6 fusion.60
  141.3 6.2 %dynamic_update_slice.34 = f32[50,26,128]{2,1,0:T(8,128)S(1)} dynamic-update-slice(f32[50,26,128]{2,1,0:T(8,128)S(1)} %fusion.57, f32[48,24,128]{2,1,0:T(8,128)} %fusion.60, s32[]{:T(128)} %constant.7.clone.1, s32[]{:T(128)} %constant.6.clone.1, s32[]{:T(128)} %constant.5.clone.1) | dynamic-update-slice | bytes 1179652 | tf_op jit(solution)/shard_map/dynamic_update_slice | solution.py:47
  147.6 2.6 fusion.63
  150.1 6.2 %dynamic_update_slice.35 = f32[50,26,128]{2,1,0:T(8,128)S(1)} dynamic-update-slice(f32[50,26,128]{2,1,0:T(8,128)S(1)} %dynamic_update_slice.34, f32[48,24,128]{2,1,0:T(8,128)} %fusion.63, s32[]{:T(128)} %constant.7.clone.1, s32[]{:T(128)} %constant.7.clone.1, s32[]{:T(128)} %constant.5.clone.1) | dynamic-update-slice | bytes 1179652 | tf_op jit(solution)/shard_map/dynamic_update_slice | solution.py:47
  157.1 40.0 %all-reduce.4.cloned.1.call-done = f32[1024,3,3,128]{3,0,2,1:T(8,128)} async-done(((f32[1024,3,3,128]{3,0,2,1:T(8,128)}), f32[1024,3,3,128]{3,0,2,1:T(8,128)}) %all-reduce.4.cloned.1.call-update) | async-done | bytes 4718608 | tf_op jit(solution)/shard_map/psum | solution.py:61
  197.2 1.6 dynamic-slice_multiply_fusion
  198.8 61.2 %reduce-scatter.2.cloned.1.call-done = f32[6,24,1024]{2,1,0:T(8,128)} async-done(((f32[48,24,1024]{2,1,0:T(8,128)}), f32[6,24,1024]{2,1,0:T(8,128)}) %reduce-scatter.2.cloned.1.call-update) | async-done | bytes 589840 | tf_op jit(solution)/shard_map/reduce_scatter | solution.py:29
  259.9 1.8 convert_bitcast_fusion
  (29 shorter events, 11.2 us)
Async XLA Ops:
  7.2 45.1 %all-gather.2.cloned.1.call-start = ((), (), s32[]{:S(2)}) async-start(), calls=%async_computation.2 | async-start | bytes 2654208 | tf_op jit(solution)/shard_map/all_gather | solution.py:38
  7.9 189.3 %all-reduce.4.cloned.1.call-start = ((), (), s32[]{:S(2)}) async-start(), calls=%async_computation.3 | async-start | bytes 9437184 | tf_op jit(solution)/shard_map/psum | solution.py:61
  7.9 4.1 %copy-start.1 = (bf16[1,48,24,128]{3,2,1,0:T(8,128)(2,1)S(1)}, bf16[1,48,24,128]{3,2,1,0:T(8,128)(2,1)}, u32[]{:S(2)}) copy-start(bf16[1,48,24,128]{3,2,1,0:T(8,128)(2,1)} %param.3) | copy-start | bytes 884740
  52.3 3.2 %copy-start = (bf16[1,48,24,1024]{3,2,0,1:T(8,128)(2,1)S(1)}, bf16[1,48,24,1024]{3,2,0,1:T(8,128)(2,1)}, u32[]{:S(2)}) copy-start(bf16[1,48,24,1024]{3,2,0,1:T(8,128)(2,1)} %all-gather.2.cloned.1.call-done) | copy-start | bytes 7077892
  72.3 187.6 %reduce-scatter.2.cloned.1.call-start = ((), (), s32[]{:S(2)}) async-start(), calls=%async_computation.1 | async-start | bytes 5308416 | tf_op jit(solution)/shard_map/reduce_scatter | solution.py:29
  72.4 12.2 %slice-start = ((s8[4718592]{0:T(1024)(128)(4,1)}), s8[4194304]{0:T(1024)(128)(4,1)S(1)}, s32[]{:S(2)}) async-start(s8[4718592]{0:T(1024)(128)(4,1)} %bitcast.252), calls=%async_computation.4 | async-start | bytes 8388608
  72.4 12.2 %slice-start.2 = ((s8[4718592]{0:T(1024)(128)(4,1)}), s8[4194304]{0:T(1024)(128)(4,1)S(1)}, s32[]{:S(2)}) async-start(s8[4718592]{0:T(1024)(128)(4,1)} %bitcast.254), calls=%async_computation.6 | async-start | bytes 8388608
  76.6 8.0 %slice-start.1 = ((s8[4718592]{0:T(1024)(128)(4,1)}), s8[524288]{0:T(1024)(128)(4,1)S(1)}, s32[]{:S(2)}) async-start(s8[4718592]{0:T(1024)(128)(4,1)} %bitcast.252), calls=%async_computation.5 | async-start | bytes 1048576
  76.6 8.0 %slice-start.3 = ((s8[4718592]{0:T(1024)(128)(4,1)}), s8[524288]{0:T(1024)(128)(4,1)S(1)}, s32[]{:S(2)}) async-start(s8[4718592]{0:T(1024)(128)(4,1)} %bitcast.254), calls=%async_computation.7 | async-start | bytes 1048576
Sparse Core Ops, SparseCore 0:
  9.8 42.4 all-gather.1
  72.5 124.6 all-reduce.3
  199.9 59.9 reduce-scatter.1
where the time goes:
time: 270 us; the launch traced here: 268 us
  waiting for transfers between devices  127 us (47%)
  matrix products  79.7 us (30%)
  local copies, waits for them, and re-layouts  44.6 us (17%)
  between operations  13.9 us (5%)
  other arithmetic  3.4 us (1%)
    reduce_scatter x1, waiting for transfers between devices, on_device(): lax.psum_scatter(conv_rows(xpad, kernel, my_rows * lax.axis_size('filter'...  61.2 us
    dot_general x9, matrix products, conv_rows(): jnp.einsum('hwi,io->hwo', xpad[a:a + count, b:b + width], weights[a, b],...  44.8 us
    psum x1, waiting for transfers between devices, on_device(): whole = lax.psum(grads, 'dp')  40 us
    dynamic_update_slice x7, local copies, waits for them, and re-layouts, on_device(): lax.dynamic_update_slice(back_pad, region + contrib, (start + a, b, 0))  37.7 us
    all_gather x1, waiting for transfers between devices, on_device(): grad_rows = lax.all_gather(cotangent, 'filter', axis=1, tiled=True)[0]  24.7 us
    dot_general x9, matrix products, on_device(): jnp.einsum('hwo,io->hwi', grad_rows, kernel[a, b], preferred_element_type...  20.9 us
    dot_general x9, matrix products, on_device(): jnp.einsum('hwi,hwo->oi', xpad[a:a + count, b:b + width], grad_rows, pref...  14 us
    reshape x1, local copies, waits for them, and re-layouts, on_device(): grads = jnp.stack(taps, 1).reshape(channels, 3, 3, local_in)  6.04 us
  transfers between devices with their start and end apart: 3, of which 3 were waited for; matrix products, arithmetic and copies ran while one was open for 39% of the time, Pallas kernels for 0%

commit v1 on v0

--- a/solution.py
+++ b/solution.py
@@ -2,6 +2,22 @@
 import jax.numpy as jnp
 from jax import lax
 from jax.sharding import PartitionSpec as P
+
+
+def ring_gather(x, axis, dim):
+    ways, here, step = (lax.axis_size(axis), lax.axis_index(axis), x.shape[dim])
+    lengths = [n * ways if d == dim else n for d, n in enumerate(x.shape)]
+    full = lax.dynamic_update_slice_in_dim(jnp.zeros(lengths, x.dtype), x, here * step, axis=dim)
+    going_up = going_down = x
+    for far in range(1, ways // 2 + 1):
+        going_up = lax.ppermute(going_up, axis, [(d, (d + 1) % ways) for d in range(ways)])
+        full = lax.dynamic_update_slice_in_dim(full, going_up, (here - far) % ways * step, axis=dim)
+        if 2 * far < ways:
+            going_down = lax.ppermute(going_down, axis, [(d, (d - 1) % ways) for d in range(ways)])
+            full = lax.dynamic_update_slice_in_dim(
+                full, going_down, (here + far) % ways * step, axis=dim
+            )
+    return full
 
 
 def conv_rows(xpad, weights, count, width):
@@ -35,7 +51,7 @@
     outputs = summed.astype(jnp.bfloat16)[None]
     start = jnp.int32(0)
     back_pad = jnp.zeros((height + 2, width + 2, local_in), jnp.float32)
-    grad_rows = lax.all_gather(cotangent, "filter", axis=1, tiled=True)[0]
+    grad_rows = ring_gather(cotangent, "filter", 1)[0]
     count = grad_rows.shape[0]
     taps = []
     for a in range(3):

time: 270 us -> 222 us (0.82)
  waiting for transfers between devices: 127 us -> 44.2 us
  local copies, waits for them, and re-layouts: 44.6 us -> 62.5 us
  starting transfers between devices: 0.12 us -> 11.9 us
  other arithmetic: 3.4 us -> 9.46 us
  matrix products: 79.7 us -> 76.1 us
    reduce_scatter x1, waiting for transfers between devices: 61.2 us -> 0.01 us  [on_device(): lax.psum_scatter(conv_rows(xpad, kernel, my_rows * lax.axis_size('filter'...]
    all_gather x1 -> x0, waiting for transfers between devices: 24.7 us -> none  [on_device(): grad_rows = lax.all_gather(cotangent, 'filter', axis=1, tiled=True)[0]]
    dynamic_update_slice x0 -> x8, local copies, waits for them, and re-layouts: none -> 12 us  [the longest x4 5.94 us: ring_gather(): lax.dynamic_update_slice_in_dim(full, going_up, (here - far) % ways * ste...]
    ppermute x0 -> x7, starting transfers between devices: none -> 11.8 us  [the longest x3 9.27 us: ring_gather(): lax.ppermute(going_down, axis, [(d, (d - 1) % ways) for d in range(ways)])]
    squeeze x0 -> x9, local copies, waits for them, and re-layouts: none -> 8.38 us  [on_device(): grad_rows = ring_gather(cotangent, 'filter', 1)[0]]
    reshape x1 -> x0, local copies, waits for them, and re-layouts: 6.04 us -> none  [on_device(): grads = jnp.stack(taps, 1).reshape(channels, 3, 3, local_in)]
    add x0 -> x6, other arithmetic: none -> 5.5 us  [on_device(): region + contrib]
    dot_general x9, matrix products: 20.9 us -> 15.6 us  [on_device(): jnp.einsum('hwo,io->hwi', grad_rows, kernel[a, b], preferred_element_type...]
  transfers between devices with their start and end apart: 3 -> 9, of which waited for: 3 -> 3; matrix products, arithmetic and copies ran while one was open for 39% -> 58% of each run, Pallas kernels for 0% -> 0%
where the time goes in v1:
time: 222 us; the launch traced here: 220 us
  matrix products  76.1 us (34%)
  local copies, waits for them, and re-layouts  62.5 us (28%)
  waiting for transfers between devices  44.2 us (20%)
  between operations  15.9 us (7%)
  starting transfers between devices  11.9 us (5%)
  other arithmetic  9.46 us (4%)
    dot_general x9, matrix products, conv_rows(): jnp.einsum('hwi,io->hwo', xpad[a:a + count, b:b + width], weights[a, b],...  45 us
    psum x1, waiting for transfers between devices, on_device(): whole = lax.psum(grads, 'dp')  40.4 us
    dynamic_update_slice x7, local copies, waits for them, and re-layouts, on_device(): lax.dynamic_update_slice(back_pad, region + contrib, (start + a, b, 0))  37 us
    dot_general x9, matrix products, on_device(): jnp.einsum('hwo,io->hwi', grad_rows, kernel[a, b], preferred_element_type...  15.6 us
    dot_general x9, matrix products, on_device(): jnp.einsum('hwi,hwo->oi', xpad[a:a + count, b:b + width], grad_rows, pref...  15.5 us
    ppermute x3, starting transfers between devices, ring_gather(): lax.ppermute(going_down, axis, [(d, (d - 1) % ways) for d in range(ways)])  9.27 us
    squeeze x9, local copies, waits for them, and re-layouts, on_device(): grad_rows = ring_gather(cotangent, 'filter', 1)[0]  8.38 us
    dynamic_update_slice x4, local copies, waits for them, and re-layouts, ring_gather(): lax.dynamic_update_slice_in_dim(full, going_up, (here - far) % ways * ste...  5.94 us
  transfers between devices with their start and end apart: 9, of which 3 were waited for; matrix products, arithmetic and copies ran while one was open for 58% of the time, Pallas kernels for 0%

profile of v1, /device:TPU:1, one launch (start us, length us, event | category | flops | bytes accessed | tf_op | source)
XLA Modules:
  0.0 220.0 jit_solution(7705846912188126676)
XLA Ops:
  8.1 2.5 %collective-permute-start = (bf16[1,6,24,1024]{3,2,1,0:T(8,128)(2,1)}, bf16[1,6,24,1024]{3,2,1,0:T(8,128)(2,1)}, u32[]{:S(2)}, u32[]{:S(2)}) collective-permute-start(bf16[1,6,24,1024]{3,2,1,0:T(8,128)(2,1)} %param.5), channel_id=1, source_target_pairs={{0,1},{1,2},{2,3},{3,4},{4,5},{5,6},{6,7},{7,0},{8,9},{9,10},{10,1... | collective-permute-start | bytes 884744 | tf_op jit(solution)/shard_map/ppermute | solution.py:13
  10.6 4.0 %collective-permute-start.1 = (bf16[1,6,24,1024]{3,2,1,0:T(8,128)(2,1)}, bf16[1,6,24,1024]{3,2,1,0:T(8,128)(2,1)}, u32[]{:S(2)}, u32[]{:S(2)}) collective-permute-start(bf16[1,6,24,1024]{3,2,1,0:T(8,128)(2,1)} %param.5), channel_id=1, source_target_pairs={{0,7},{1,0},{2,1},{3,2},{4,3},{5,4},{6,5},{7,6},{8,15},{9,8},{10,9... | collective-permute-start | bytes 884744 | tf_op jit(solution)/shard_map/ppermute | solution.py:16
  14.6 4.1 %pad_slice_fusion = (bf16[48,24,128]{2,1,0:T(8,128)(2,1)}, bf16[48,24,128]{2,1,0:T(8,128)(2,1)}, bf16[48,24,128]{2,1,0:T(8,128)(2,1)}, bf16[48,24,128]{2,1,0:T(8...) fusion(bf16[48,24,128]{2,1,0:T(8,128)(2,1)} %bitcast.142), kind=kLoop, calls=%fused_computation.30 | loop fusion | bytes 2654208 | tf_op jit(solution)/shard_map/slice | solution.py:29
  18.7 3.9 %fusion.26 = f32[48,24,1024]{2,1,0:T(8,128)} fusion(bf16[3,3,128,1024]{3,2,1,0:T(8,128)(2,1)} %param.4, bf16[48,24,128]{2,1,0:T(8,128)(2,1)S(1)} %bitcast.143), kind=kOutput, calls=%fused_computation.54 | convolution fusion | flops 301989888 | bytes 5275648 | tf_op jit(solution)/shard_map/hwi,io->hwo/dot_general | solution.py:27
  24.7 3.9 %fusion.30 = f32[48,24,1024]{2,1,0:T(8,128)} fusion(bf16[3,3,128,1024]{3,2,1,0:T(8,128)(2,1)} %param.4, bf16[48,24,128]{2,1,0:T(8,128)(2,1)S(1)} %bitcast.144), kind=kOutput, calls=%fused_computation.58 | convolution fusion | flops 301989888 | bytes 5275648 | tf_op jit(solution)/shard_map/hwi,io->hwo/dot_general | solution.py:27
  28.6 3.9 %fusion.34 = f32[48,24,1024]{2,1,0:T(8,128)} fusion(bf16[3,3,128,1024]{3,2,1,0:T(8,128)(2,1)} %param.4, bf16[48,24,128]{2,1,0:T(8,128)(2,1)S(1)} %bitcast.145), kind=kOutput, calls=%fused_computation.62 | convolution fusion | flops 301989888 | bytes 5275648 | tf_op jit(solution)/shard_map/hwi,io->hwo/dot_general | solution.py:27
  32.5 2.7 %collective-permute-start.3 = (bf16[1,6,24,1024]{3,2,1,0:T(8,128)(2,1)}, bf16[1,6,24,1024]{3,2,1,0:T(8,128)(2,1)}, u32[]{:S(2)}, u32[]{:S(2)}) collective-permute-start(bf16[1,6,24,1024]{3,2,1,0:T(8,128)(2,1)} %collective-permute-done.1), channel_id=1, source_target_pairs={{0,7},{1,0},{2,1},{3,2},{4,3},{5,4},{6,5},{7,6},{8,15},{9,8},{10,9... | collective-permute-start | bytes 884744 | tf_op jit(solution)/shard_map/ppermute | solution.py:16
  35.2 2.4 %collective-permute-done.2 = bf16[1,6,24,1024]{3,2,1,0:T(8,128)(2,1)S(1)} collective-permute-done((bf16[1,6,24,1024]{3,2,1,0:T(8,128)(2,1)}, bf16[1,6,24,1024]{3,2,1,0:T(8,128)(2,1)S(1)}, u32[]{:S(2)}, u32[]{:S(2)}) %collective-permute-start.2) | collective-permute-done | bytes 294944 | tf_op jit(solution)/shard_map/ppermute | solution.py:13
  37.6 3.9 %fusion.42 = f32[48,24,1024]{2,1,0:T(8,128)} fusion(bf16[3,3,128,1024]{3,2,1,0:T(8,128)(2,1)} %param.4, bf16[48,24,128]{2,1,0:T(8,128)(2,1)S(1)} %bitcast.146), kind=kOutput, calls=%fused_computation.70 | convolution fusion | flops 301989888 | bytes 5275648 | tf_op jit(solution)/shard_map/hwi,io->hwo/dot_general | solution.py:27
  41.5 2.6 %collective-permute-start.5 = (bf16[1,6,24,1024]{3,2,1,0:T(8,128)(2,1)}, bf16[1,6,24,1024]{3,2,1,0:T(8,128)(2,1)}, u32[]{:S(2)}, u32[]{:S(2)}) collective-permute-start(bf16[1,6,24,1024]{3,2,1,0:T(8,128)(2,1)} %collective-permute-done.3), channel_id=1, source_target_pairs={{0,7},{1,0},{2,1},{3,2},{4,3},{5,4},{6,5},{7,6},{8,15},{9,8},{10,9... | collective-permute-start | bytes 884744 | tf_op jit(solution)/shard_map/ppermute | solution.py:16
  45.5 3.9 %fusion.46 = f32[48,24,1024]{2,1,0:T(8,128)} fusion(bf16[3,3,128,1024]{3,2,1,0:T(8,128)(2,1)} %param.4, bf16[48,24,128]{2,1,0:T(8,128)(2,1)S(1)} %bitcast.147), kind=kOutput, calls=%fused_computation.74 | convolution fusion | flops 301989888 | bytes 5275648 | tf_op jit(solution)/shard_map/hwi,io->hwo/dot_general | solution.py:27
  68.0 2.6 %fusion.8 = f32[1024,9,128]{2,0,1:T(8,128)} fusion(bf16[48,24,1024]{2,0,1:T(8,128)(2,1)S(1)} %dynamic_update_slice.66, bf16[48,24,128]{2,1,0:T(8,128)(2,1)} %get-tuple-element.10), kind=kOutput, calls=%fused_computation.18 | convolution fusion | flops 301989888 | bytes 3178496 | tf_op jit(solution)/shard_map/hwi,hwo->oi/dot_general | solution.py:65
  83.6 4.2 %fusion.54 = f32[48,24,1024]{2,1,0:T(8,128)} fusion(bf16[3,3,128,1024]{3,2,1,0:T(8,128)(2,1)} %param.4, bf16[48,24,128]{2,1,0:T(8,128)(2,1)S(1)} %bitcast.149), kind=kOutput, calls=%fused_computation.82 | convolution fusion | flops 301989888 | bytes 5275648 | tf_op jit(solution)/shard_map/hwi,io->hwo/dot_general | solution.py:27
  87.9 3.9 %fusion.50 = f32[48,24,1024]{2,1,0:T(8,128)} fusion(bf16[3,3,128,1024]{3,2,1,0:T(8,128)(2,1)} %param.4, bf16[48,24,128]{2,1,0:T(8,128)(2,1)S(1)} %bitcast.150), kind=kOutput, calls=%fused_computation.78 | convolution fusion | flops 301989888 | bytes 5275648 | tf_op jit(solution)/shard_map/hwi,io->hwo/dot_general | solution.py:27
  91.8 3.8 %fusion.38 = f32[48,24,1024]{2,1,0:T(8,128)} fusion(bf16[3,3,128,1024]{3,2,1,0:T(8,128)(2,1)} %param.4, bf16[1,48,24,128]{3,2,1,0:T(8,128)(2,1)S(1)} %copy-done), kind=kOutput, calls=%fused_computation.66 | convolution fusion | flops 301989888 | bytes 5275648 | tf_op jit(solution)/shard_map/hwi,io->hwo/dot_general | solution.py:27
  95.7 13.4 %add_add_fusion = f32[48,24,1024]{2,1,0:T(8,128)} fusion(f32[48,24,1024]{2,1,0:T(8,128)S(1)} %bitcast.153, f32[48,24,1024]{2,1,0:T(8,128)S(1)} %bitcast.155, f32[48,24,1024]{2,1,0:T(8,128)} %fusion.34, f32[48,24,1024]{2,1,0:T(8,128)} %fusion.38, f32[48,24,1024]{2,1,0:T(8,128)} %fusion.42, f32[48,24,1024]{2,1,0:T(8,128)} %fusion.46, ...), kind=kOutput, calls=%fused_computation | convolution fusion | flops 311427072 | bytes 43024384 | tf_op jit(solution)/shard_map/hwi,io->hwo/dot_general | solution.py:27
  109.1 1.7 fusion.52
  111.2 1.7 fusion.48
  113.9 6.3 %dynamic_update_slice.68 = f32[50,26,128]{2,1,0:T(8,128)S(1)} dynamic-update-slice(f32[50,26,128]{2,1,0:T(8,128)S(1)} %dynamic_update_slice.67, f32[48,24,128]{2,1,0:T(8,128)} %copy_add_fusion, s32[]{:T(128)} %constant.68.clone.1, s32[]{:T(128)} %constant.73.clone.1, s32[]{:T(128)} %constant.68.clone.1) | dynamic-update-slice | bytes 1179652 | tf_op jit(solution)/shard_map/dynamic_update_slice | solution.py:63
  120.3 1.7 fusion.44
  123.0 6.3 %dynamic_update_slice.69 = f32[50,26,128]{2,1,0:T(8,128)S(1)} dynamic-update-slice(f32[50,26,128]{2,1,0:T(8,128)S(1)} %dynamic_update_slice.68, f32[48,24,128]{2,1,0:T(8,128)} %slice_add_fusion.6, s32[]{:T(128)} %constant.68.clone.1, s32[]{:T(128)} %constant.75.clone.1, s32[]{:T(128)} %constant.68.clone.1) | dynamic-update-slice | bytes 1179652 | tf_op jit(solution)/shard_map/dynamic_update_slice | solution.py:63
  129.4 1.7 fusion.40
  131.4 1.7 fusion.36
  134.2 6.3 %dynamic_update_slice.71 = f32[50,26,128]{2,1,0:T(8,128)S(1)} dynamic-update-slice(f32[50,26,128]{2,1,0:T(8,128)S(1)} %fusion.10, f32[48,24,128]{2,1,0:T(8,128)} %slice_add_fusion.4, s32[]{:T(128)} %constant.73.clone.1, s32[]{:T(128)} %constant.73.clone.1, s32[]{:T(128)} %constant.68.clone.1) | dynamic-update-slice | bytes 1179652 | tf_op jit(solution)/shard_map/dynamic_update_slice | solution.py:63
  140.4 1.7 fusion.32
  143.2 6.3 %dynamic_update_slice.72 = f32[50,26,128]{2,1,0:T(8,128)S(1)} dynamic-update-slice(f32[50,26,128]{2,1,0:T(8,128)S(1)} %dynamic_update_slice.71, f32[48,24,128]{2,1,0:T(8,128)} %slice_add_fusion.3, s32[]{:T(128)} %constant.73.clone.1, s32[]{:T(128)} %constant.75.clone.1, s32[]{:T(128)} %constant.68.clone.1) | dynamic-update-slice | bytes 1179652 | tf_op jit(solution)/shard_map/dynamic_update_slice | solution.py:63
  149.5 1.7 fusion.28
  154.3 6.2 %dynamic_update_slice.74 = f32[50,26,128]{2,1,0:T(8,128)S(1)} dynamic-update-slice(f32[50,26,128]{2,1,0:T(8,128)S(1)} %fusion.9, f32[48,24,128]{2,1,0:T(8,128)} %slice_add_fusion.1, s32[]{:T(128)} %constant.75.clone.1, s32[]{:T(128)} %constant.73.clone.1, s32[]{:T(128)} %constant.68.clone.1) | dynamic-update-slice | bytes 1179652 | tf_op jit(solution)/shard_map/dynamic_update_slice | solution.py:63
  160.5 1.7 fusion.21
  162.5 5.5 %dynamic_update_slice.75 = f32[50,26,128]{2,1,0:T(8,128)S(1)} dynamic-update-slice(f32[50,26,128]{2,1,0:T(8,128)S(1)} %dynamic_update_slice.74, f32[48,24,128]{2,1,0:T(8,128)S(1)} %slice_add_fusion, s32[]{:T(128)} %constant.75.clone.1, s32[]{:T(128)} %constant.75.clone.1, s32[]{:T(128)} %constant.68.clone.1) | dynamic-update-slice | bytes 1179652 | tf_op jit(solution)/shard_map/dynamic_update_slice | solution.py:63
  168.8 40.4 %all-reduce.4.cloned.1.call-done = f32[1024,3,3,128]{3,0,2,1:T(8,128)} async-done(((f32[1024,3,3,128]{3,0,2,1:T(8,128)}), f32[1024,3,3,128]{3,0,2,1:T(8,128)}) %all-reduce.4.cloned.1.call-update) | async-done | bytes 4718608 | tf_op jit(solution)/shard_map/psum | solution.py:77
  210.8 1.8 convert_bitcast_fusion
  (82 shorter events, 45.4 us)
Async XLA Ops:
  8.0 10.7 %copy-start = (bf16[1,48,24,128]{3,2,1,0:T(8,128)(2,1)S(1)}, bf16[1,48,24,128]{3,2,1,0:T(8,128)(2,1)}, u32[]{:S(2)}) copy-start(bf16[1,48,24,128]{3,2,1,0:T(8,128)(2,1)} %param.3) | copy-start | bytes 884740
  8.0 201.2 %all-reduce.4.cloned.1.call-start = ((), (), s32[]{:S(2)}) async-start(), calls=%async_computation.2 | async-start | bytes 9437184 | tf_op jit(solution)/shard_map/psum | solution.py:77
  8.1 20.5 %collective-permute-start = (bf16[1,6,24,1024]{3,2,1,0:T(8,128)(2,1)}, bf16[1,6,24,1024]{3,2,1,0:T(8,128)(2,1)}, u32[]{:S(2)}, u32[]{:S(2)}) collective-permute-start(bf16[1,6,24,1024]{3,2,1,0:T(8,128)(2,1)} %param.5), channel_id=1, source_target_pairs={{0,1},{1,2},{2,3},{3,4},{4,5},{5,6},{6,7},{7,0},{8,9},{9,10},{10,1... | collective-permute-start | bytes 884744 | tf_op jit(solution)/shard_map/ppermute | solution.py:13
  10.6 21.9 %collective-permute-start.1 = (bf16[1,6,24,1024]{3,2,1,0:T(8,128)(2,1)}, bf16[1,6,24,1024]{3,2,1,0:T(8,128)(2,1)}, u32[]{:S(2)}, u32[]{:S(2)}) collective-permute-start(bf16[1,6,24,1024]{3,2,1,0:T(8,128)(2,1)} %param.5), channel_id=1, source_target_pairs={{0,7},{1,0},{2,1},{3,2},{4,3},{5,4},{6,5},{7,6},{8,15},{9,8},{10,9... | collective-permute-start | bytes 884744 | tf_op jit(solution)/shard_map/ppermute | solution.py:16
  18.7 3.9 %copy-start.1 = (bf16[1,6,24,1024]{3,2,1,0:T(8,128)(2,1)S(1)}, bf16[1,6,24,1024]{3,2,1,0:T(8,128)(2,1)}, u32[]{:S(2)}) copy-start(bf16[1,6,24,1024]{3,2,1,0:T(8,128)(2,1)} %param.5) | copy-start | bytes 884740
  28.6 9.0 %collective-permute-start.2 = (bf16[1,6,24,1024]{3,2,1,0:T(8,128)(2,1)}, bf16[1,6,24,1024]{3,2,1,0:T(8,128)(2,1)S(1)}, u32[]{:S(2)}, u32[]{:S(2)}) collective-permute-start(bf16[1,6,24,1024]{3,2,1,0:T(8,128)(2,1)} %collective-permute-done), channel_id=1, source_target_pairs={{0,1},{1,2},{2,3},{3,4},{4,5},{5,6},{6,7},{7,0},{8,9},{9,10},{10,1... | collective-permute-start | bytes 884744 | tf_op jit(solution)/shard_map/ppermute | solution.py:13
  32.5 9.0 %collective-permute-start.3 = (bf16[1,6,24,1024]{3,2,1,0:T(8,128)(2,1)}, bf16[1,6,24,1024]{3,2,1,0:T(8,128)(2,1)}, u32[]{:S(2)}, u32[]{:S(2)}) collective-permute-start(bf16[1,6,24,1024]{3,2,1,0:T(8,128)(2,1)} %collective-permute-done.1), channel_id=1, source_target_pairs={{0,7},{1,0},{2,1},{3,2},{4,3},{5,4},{6,5},{7,6},{8,15},{9,8},{10,9... | collective-permute-start | bytes 884744 | tf_op jit(solution)/shard_map/ppermute | solution.py:16
  37.6 3.9 %copy-start.9 = (bf16[1,6,24,1024]{3,2,1,0:T(8,128)(2,1)}, bf16[1,6,24,1024]{3,2,1,0:T(8,128)(2,1)S(1)}, u32[]{:S(2)}) copy-start(bf16[1,6,24,1024]{3,2,1,0:T(8,128)(2,1)S(1)} %collective-permute-done.2) | copy-start | bytes 884740
  37.6 8.0 %collective-permute-start.4 = (bf16[1,6,24,1024]{3,2,1,0:T(8,128)(2,1)S(1)}, bf16[1,6,24,1024]{3,2,1,0:T(8,128)(2,1)}, u32[]{:S(2)}, u32[]{:S(2)}) collective-permute-start(bf16[1,6,24,1024]{3,2,1,0:T(8,128)(2,1)S(1)} %collective-permute-done.2), channel_id=1, source_target_pairs={{0,1},{1,2},{2,3},{3,4},{4,5},{5,6},{6,7},{7,0},{8,9},{9,10},{10,1... | collective-permute-start | bytes 884744 | tf_op jit(solution)/shard_map/ppermute | solution.py:13
  41.5 19.6 %collective-permute-start.5 = (bf16[1,6,24,1024]{3,2,1,0:T(8,128)(2,1)}, bf16[1,6,24,1024]{3,2,1,0:T(8,128)(2,1)}, u32[]{:S(2)}, u32[]{:S(2)}) collective-permute-start(bf16[1,6,24,1024]{3,2,1,0:T(8,128)(2,1)} %collective-permute-done.3), channel_id=1, source_target_pairs={{0,7},{1,0},{2,1},{3,2},{4,3},{5,4},{6,5},{7,6},{8,15},{9,8},{10,9... | collective-permute-start | bytes 884744 | tf_op jit(solution)/shard_map/ppermute | solution.py:16
  45.5 19.8 %collective-permute-start.6 = (bf16[1,6,24,1024]{3,2,1,0:T(8,128)(2,1)}, bf16[1,6,24,1024]{3,2,1,0:T(8,128)(2,1)}, u32[]{:S(2)}, u32[]{:S(2)}) collective-permute-start(bf16[1,6,24,1024]{3,2,1,0:T(8,128)(2,1)} %collective-permute-done.4), channel_id=1, source_target_pairs={{0,1},{1,2},{2,3},{3,4},{4,5},{5,6},{6,7},{7,0},{8,9},{9,10},{10,1... | collective-permute-start | bytes 884744 | tf_op jit(solution)/shard_map/ppermute | solution.py:13
  68.0 2.6 %copy-start.8 = (bf16[48,24,128]{2,1,0:T(8,128)(2,1)S(1)}, bf16[48,24,128]{2,1,0:T(8,128)(2,1)}, u32[]{:S(2)}) copy-start(bf16[48,24,128]{2,1,0:T(8,128)(2,1)} %get-tuple-element.9) | copy-start | bytes 884740
  70.6 1.6 copy-start.7
  72.2 1.6 copy-start.6
  75.5 1.6 copy-start.5
  77.1 1.6 copy-start.4
  78.7 1.6 copy-start.3
  80.3 1.6 copy-start.2
  83.6 127.2 %reduce-scatter.2.cloned.1.call-start = ((), (), s32[]{:S(2)}) async-start(), calls=%async_computation.1 | async-start | bytes 5308416 | tf_op jit(solution)/shard_map/reduce_scatter | solution.py:45
  83.6 12.0 %slice-start = ((s8[4718592]{0:T(1024)(128)(4,1)}), s8[4194304]{0:T(1024)(128)(4,1)S(1)}, s32[]{:S(2)}) async-start(s8[4718592]{0:T(1024)(128)(4,1)} %bitcast.152), calls=%async_computation.3 | async-start | bytes 8388608
  83.6 12.0 %slice-start.2 = ((s8[4718592]{0:T(1024)(128)(4,1)}), s8[4194304]{0:T(1024)(128)(4,1)S(1)}, s32[]{:S(2)}) async-start(s8[4718592]{0:T(1024)(128)(4,1)} %bitcast.154), calls=%async_computation.5 | async-start | bytes 8388608
  87.8 7.8 %slice-start.1 = ((s8[4718592]{0:T(1024)(128)(4,1)}), s8[524288]{0:T(1024)(128)(4,1)S(1)}, s32[]{:S(2)}) async-start(s8[4718592]{0:T(1024)(128)(4,1)} %bitcast.152), calls=%async_computation.4 | async-start | bytes 1048576
  87.9 7.8 %slice-start.3 = ((s8[4718592]{0:T(1024)(128)(4,1)}), s8[524288]{0:T(1024)(128)(4,1)S(1)}, s32[]{:S(2)}) async-start(s8[4718592]{0:T(1024)(128)(4,1)} %bitcast.154), calls=%async_computation.6 | async-start | bytes 1048576
Sparse Core Ops, SparseCore 0:
  83.7 125.4 all-reduce.3
Sparse Core Ops, SparseCore 1:
  109.2 62.4 reduce-scatter.1
